TPU v7x, 32 devices: a whole 2x2x4 slice. The times are simulated.
32 devices in a mesh: vis: 8 (over y, x, core), wav: 4 (over z).
Axes of the slice: x: 2, y: 2, z: 4, core: 2. Of those that a mesh axis runs over, the one named last changes fastest.
Arguments:
- image: float32 [4096, 4096], P('vis', 'wav'), may hold values from -6 to 6
- kernel_v: bfloat16 [1024, 64, 256], P(('vis', 'wav')), may hold values from -0.5 to 0.5
- kernel_u: bfloat16 [1024, 64, 256], P(('vis', 'wav')), may hold values from -0.5 to 0.5
- measured: bfloat16 [1024, 2, 256], P(('vis', 'wav')), may hold values from -4 to 4
- dest_owner: int32 [1024, 1], P(('vis', 'wav')), may hold values from 0 to 7; in each aligned block of 32 rows (0 to 31, 32 to 63, ...) at most 8 rows name the same one
- patch_slot: int32 [1024], P(('vis', 'wav')), may hold values from 0 to 127
- thresholds: float32 [4], replicated, may hold values from 0.1 to 1
Outputs:
- restored: float32 [4096, 4096], P('vis', 'wav')
- residual: float32 [1024, 2, 256], P(('vis', 'wav'))
Inputs may be any that keep to these rules, and one draw needn't show every extreme that they name: `dest_owner`: the vis index of the owner of the block's uv cells; the 32 blocks of one device name one owner at most 8 times, a bound that some block reaches. `patch_slot`: the block's kernel block among the 128 of its owner's tile in the band of the block's wav index.
All inputs are finite; a program needn't handle non-finite values.
Results may differ from a plain program's by a relative error of at most 0.0017.
Values may be sent and summed in bfloat16 or wider, within the bound.
No kernel may reach another device: no remote copies, remote signals or barrier semaphores. Data moves between devices by JAX's collectives and lax.ppermute only.
A program may use at most 128 MiB of HBM per device.

v0:
```python
import math
import jax
import jax.numpy as jnp
import numpy as np
from jax import lax
from jax.sharding import PartitionSpec as P

IMG = 4096
PATCH = 64
FA = 64
FB = 64
HIGHEST = lax.Precision.HIGHEST


def haar_table():
    rows = np.zeros((8, 8))
    root = 1.0 / np.sqrt(8.0)
    rows[0, :] = root
    rows[1, :4] = root
    rows[1, 4:] = -root
    rows[2, 0:2] = 0.5
    rows[2, 2:4] = -0.5
    rows[3, 4:6] = 0.5
    rows[3, 6:8] = -0.5
    for index in range(4):
        rows[4 + index, 2 * index] = np.sqrt(0.5)
        rows[4 + index, 2 * index + 1] = -np.sqrt(0.5)
    return np.kron(np.eye(16), rows)


def basis_prox(field, shift, limit, table):
    height, width = field.shape
    moved = jnp.roll(field, -shift, axis=1).reshape(height, width // 128, 128)
    coeff = jnp.einsum("rgj,kj->rgk", moved, table, precision=HIGHEST)
    coeff = coeff.reshape(height // 2, 2, width // 128, 128)
    factor = math.sqrt(0.5)
    upper = (coeff[:, 0] + coeff[:, 1]) * factor
    lower = (coeff[:, 0] - coeff[:, 1]) * factor
    upper = upper - jnp.clip(upper, -limit, limit)
    lower = lower - jnp.clip(lower, -limit, limit)
    coeff = jnp.stack([(upper + lower) * factor, (upper - lower) * factor], 1)
    coeff = coeff.reshape(height, width // 128, 128)
    back = jnp.einsum("rgk,kj->rgj", coeff, table, precision=HIGHEST)
    return jnp.roll(back.reshape(height, width), shift, axis=1)


def dft_tables(sign):
    first_idx = jnp.arange(FA, dtype=jnp.int32)
    second_idx = jnp.arange(FB, dtype=jnp.int32)
    first_angle = (first_idx[:, None] * first_idx[None, :] % FA).astype(jnp.float32) * (
        2.0 * math.pi / FA
    )
    twist_angle = (first_idx[:, None] * second_idx[None, :] % IMG).astype(jnp.float32) * (
        2.0 * math.pi / IMG
    )
    second_angle = (second_idx[:, None] * second_idx[None, :] % FB).astype(jnp.float32) * (
        2.0 * math.pi / FB
    )
    return (
        jnp.cos(first_angle),
        sign * jnp.sin(first_angle),
        jnp.cos(twist_angle),
        sign * jnp.sin(twist_angle),
        jnp.cos(second_angle),
        sign * jnp.sin(second_angle),
    )


def dft_last(real_part, imag_part, tables, want_imag):
    first_cos, first_sin, twist_cos, twist_sin, second_cos, second_sin = tables
    leading = real_part.shape[:-1]
    real_in = real_part.reshape(leading + (FA, FB))
    mix_real = jnp.einsum("ka,...ab->...kb", first_cos, real_in, precision=HIGHEST)
    mix_imag = jnp.einsum("ka,...ab->...kb", first_sin, real_in, precision=HIGHEST)
    if imag_part is not None:
        imag_in = imag_part.reshape(leading + (FA, FB))
        mix_real = mix_real - jnp.einsum("ka,...ab->...kb", first_sin, imag_in, precision=HIGHEST)
        mix_imag = mix_imag + jnp.einsum("ka,...ab->...kb", first_cos, imag_in, precision=HIGHEST)
    turned_real = mix_real * twist_cos - mix_imag * twist_sin
    turned_imag = mix_real * twist_sin + mix_imag * twist_cos
    factor = 1.0 / math.sqrt(IMG)
    out_real = jnp.einsum("...kb,jb->...jk", turned_real, second_cos, precision=HIGHEST)
    out_real = out_real - jnp.einsum("...kb,jb->...jk", turned_imag, second_sin, precision=HIGHEST)
    out_real = out_real.reshape(leading + (IMG,)) * factor
    if not want_imag:
        return (out_real, None)
    out_imag = jnp.einsum("...kb,jb->...jk", turned_real, second_sin, precision=HIGHEST)
    out_imag = out_imag + jnp.einsum("...kb,jb->...jk", turned_imag, second_cos, precision=HIGHEST)
    return (out_real, out_imag.reshape(leading + (IMG,)) * factor)


def degrid_values(v_side_length, u_side_length, grid_patch, measurements):
    product = jnp.einsum(
        "nac,nat->nct", grid_patch, v_side_length, preferred_element_type=jnp.float32
    )
    width = u_side_length.shape[1]
    sky_model_real = jnp.sum(product[:, :width] * u_side_length, 1)
    sky_model_imag = jnp.sum(product[:, width:] * u_side_length, 1)
    return jnp.stack([sky_model_real, sky_model_imag], 1) - measurements.astype(jnp.float32)


def grid_terms(v_side_length, u_side_length, misfit):
    weighted = jnp.concatenate(
        [misfit[:, 0, None, :] * u_side_length, misfit[:, 1, None, :] * u_side_length], 1
    ).astype(jnp.bfloat16)
    return jnp.einsum("nat,nct->nac", v_side_length, weighted, preferred_element_type=jnp.float32)


def shards(image, kernel_v, kernel_u, measured, dest_owner, patch_slot, thresholds):
    vis_count = lax.axis_size("vis")
    wav_count = lax.axis_size("wav")
    block_count = kernel_v.shape[0]
    capacity = 2 * block_count // vis_count
    slot_total = capacity * vis_count
    strip = IMG // (vis_count * wav_count)
    kv_size = IMG // vis_count
    ku_size = IMG // wav_count
    tile_down = kv_size // PATCH
    tile_across = ku_size // PATCH
    patch_count = tile_down * tile_across
    table = jnp.asarray(haar_table(), jnp.float32)
    forward_tables = dft_tables(-1.0)
    inverse_tables = dft_tables(1.0)
    target_device = dest_owner[:, 0]
    member = (target_device[:, None] == jnp.arange(vis_count, dtype=jnp.int32)[None, :]).astype(
        jnp.int32
    )
    earlier = jnp.cumsum(member, axis=0) - member
    position = target_device * capacity + jnp.sum(earlier * member, axis=1)
    slot_ids = (
        jnp.zeros((slot_total, 1), jnp.bfloat16)
        .at[position]
        .set(patch_slot[:, None].astype(jnp.bfloat16))
    )
    pack_v = jnp.zeros((slot_total,) + kernel_v.shape[1:], jnp.bfloat16).at[position].set(kernel_v)
    pack_u = jnp.zeros((slot_total,) + kernel_u.shape[1:], jnp.bfloat16).at[position].set(kernel_u)
    packed_measurements = (
        jnp.zeros((slot_total,) + measured.shape[1:], jnp.bfloat16).at[position].set(measured)
    )
    received_v_coords, received_u_coords, received_measurements, received_ids = (
        lax.all_to_all(pack_v, "vis", split_axis=0, concat_axis=0, tiled=True),
        lax.all_to_all(pack_u, "vis", split_axis=0, concat_axis=0, tiled=True),
        lax.all_to_all(packed_measurements, "vis", split_axis=0, concat_axis=0, tiled=True),
        lax.all_to_all(slot_ids, "vis", split_axis=0, concat_axis=0, tiled=True),
    )
    owning_device_ids = received_ids[:, 0].astype(jnp.int32)
    misfit = None
    estimate = image
    wav_index = lax.axis_index("wav")
    real_part, imag_part = dft_last(
        lax.all_to_all(estimate, "wav", split_axis=0, concat_axis=1, tiled=True),
        None,
        forward_tables,
        True,
    )
    stacked = jnp.stack([real_part, imag_part], 0)
    moved = lax.all_to_all(
        lax.all_to_all(stacked, "vis", split_axis=2, concat_axis=1, tiled=True),
        "wav",
        split_axis=2,
        concat_axis=1,
        tiled=True,
    )
    moved = (
        moved.reshape(2, wav_count, vis_count, strip, strip)
        .transpose(0, 4, 2, 1, 3)
        .reshape(2, strip, IMG)
    )
    real_part, imag_part = dft_last(moved[0], moved[1], forward_tables, True)
    blocks = (
        lax.all_to_all(
            jnp.stack([real_part, imag_part], 0).astype(jnp.bfloat16),
            "wav",
            split_axis=2,
            concat_axis=1,
            tiled=True,
        )
        .astype(jnp.float32)
        .reshape(2, tile_down, PATCH, tile_across, PATCH)
        .transpose(1, 3, 2, 0, 4)
    )
    misfit = degrid_values(
        received_v_coords,
        received_u_coords,
        blocks.reshape(patch_count, PATCH, 2 * PATCH).astype(jnp.bfloat16)[owning_device_ids],
        received_measurements,
    )
    onehot = (
        owning_device_ids[:, None] == jnp.arange(patch_count, dtype=jnp.int32)[None, :]
    ).astype(jnp.float32)
    summed = jnp.einsum(
        "sq,sac->qac",
        onehot,
        grid_terms(received_v_coords, received_u_coords, misfit),
        precision=HIGHEST,
    )
    blocks = summed.reshape(tile_down, tile_across, PATCH, 2, PATCH).transpose(3, 0, 2, 1, 4)
    grid_grad = blocks.reshape(2, kv_size, ku_size)
    moved = lax.all_to_all(
        grid_grad.astype(jnp.bfloat16), "wav", split_axis=1, concat_axis=2, tiled=True
    ).astype(grid_grad.dtype)
    real_part, imag_part = dft_last(moved[0], moved[1], inverse_tables, True)
    stacked = jnp.stack([real_part, imag_part], 0).transpose(0, 2, 1)
    moved = lax.all_to_all(
        lax.all_to_all(
            stacked.astype(jnp.bfloat16), "vis", split_axis=1, concat_axis=2, tiled=True
        ),
        "wav",
        split_axis=1,
        concat_axis=2,
        tiled=True,
    ).astype(stacked.dtype)
    moved = (
        moved.reshape(2, strip, wav_count, vis_count, strip)
        .transpose(0, 1, 3, 2, 4)
        .reshape(2, strip, IMG)
    )
    gradient = lax.all_to_all(
        dft_last(moved[0], moved[1], inverse_tables, False)[0].astype(jnp.bfloat16),
        "wav",
        split_axis=1,
        concat_axis=0,
        tiled=True,
    ).astype(jnp.float32)
    gathered = lax.all_gather(estimate - gradient, "wav", axis=1, tiled=True)
    single = basis_prox(gathered, wav_index, thresholds[wav_index], table)
    estimate = lax.psum_scatter(single, "wav", scatter_dimension=1, tiled=True) * (1.0 / wav_count)
    returned = lax.all_to_all(misfit, "vis", split_axis=0, concat_axis=0, tiled=True)
    residual = returned[position]
    return (estimate, residual)


def solution(mesh):
    in_specs = (
        P("vis", "wav"),
        P(("vis", "wav"), None, None),
        P(("vis", "wav"), None, None),
        P(("vis", "wav"), None, None),
        P(("vis", "wav"), None),
        P(("vis", "wav")),
        P(),
    )
    out_specs = (P("vis", "wav"), P(("vis", "wav"), None, None))
    return jax.shard_map(shards, mesh=mesh, in_specs=in_specs, out_specs=out_specs, check_vma=False)
```

profile of v0, /device:TPU:0, one launch (start us, length us, event | category | flops | bytes accessed | tf_op | source)
XLA Modules:
  0.0 1095.0 jit_solution(5774231187537844015)
XLA Ops:
  7.2 6.4 all-to-all-start.2
  14.0 47.7 %all-to-all-done.2 = f32[4,128,1024]{2,1,0:T(8,128)S(1)} async-done(((f32[4,128,1024]{2,1,0:T(8,128)}), f32[4,128,1024]{2,1,0:T(8,128)S(1)}, u32[]{:S(2)}, u32[]{:S(2)}) %all-to-all-start.2) | async-done | bytes 2097184 | tf_op jit(solution)/shard_map/all_to_all | solution.py:151
  68.1 4.2 subtract_bitcast_fusion
  75.4 3.4 fusion.53
  78.8 3.2 multiply_bitcast_fusion.1
  82.0 3.3 multiply_bitcast_fusion
  88.0 15.6 %copy.220 = f32[2,128,4096]{1,0,2:T(2,128)S(1)} copy(f32[2,128,4096]{1,2,0:T(8,128)S(1)} %pad_maximum_fusion.1) | data formatting | bytes 8388608 | tf_op jit(solution)/shard_map/stack | solution.py:156
  103.6 52.6 %all_to_all.146 = f32[2,128,4096]{1,0,2:T(2,128)S(1)} all-to-all(f32[2,128,4096]{1,0,2:T(2,128)S(1)} %copy.220), channel_id=1, replica_groups=mesh['vis'=8,'wav'=4] {'vis'}, dimensions={2} | all-to-all | bytes 8388608 | tf_op jit(solution)/shard_map/all_to_all | solution.py:158
  158.5 5.3 copy.222
  163.8 7.4 copy.223
  171.2 5.0 all-to-all-start.4
  176.6 10.1 scatter_custom_fusion
  189.3 79.8 %all-to-all-done.4 = f32[2,1024,512]{1,0,2:T(2,128)} async-done(((f32[2,1024,512]{1,0,2:T(2,128)}), f32[2,1024,512]{1,0,2:T(2,128)}, u32[]{:S(2)}, u32[]{:S(2)}) %all-to-all-start.4) | async-done | bytes 4194336 | tf_op jit(solution)/shard_map/all_to_all | solution.py:157
  269.1 3.3 all-to-all-start
  272.4 5.5 copy.224
  278.0 5.3 copy.225
  286.2 3.3 fusion.43
  289.5 3.3 fusion.45
  293.1 3.4 fusion.70
  296.5 6.3 fusion.19
  302.7 4.4 all-to-all-start.1
  307.1 4.6 fusion.35
  311.8 3.2 fusion.89
  319.7 3.7 fusion.86
  324.3 18.1 %copy.240 = bf16[2,128,4096]{1,0,2:T(2,128)(2,1)} copy(bf16[2,128,4096]{1,2,0:T(8,128)(2,1)S(1)} %pad_maximum_fusion.2) | data formatting | bytes 4194304 | tf_op jit(solution)/shard_map/stack | solution.py:172
  342.4 4.5 all-to-all-start.5
  351.0 44.9 %all-to-all-done.5 = bf16[2,128,4096]{1,0,2:T(2,128)(2,1)} async-done(((bf16[2,128,4096]{1,0,2:T(2,128)(2,1)}), bf16[2,128,4096]{1,0,2:T(2,128)(2,1)}, u32[]{:S(2)}, u32[]{:S(2)}) %all-to-all-start.5) | async-done | bytes 2097184 | tf_op jit(solution)/shard_map/all_to_all | solution.py:171
  395.9 4.1 all-to-all-start.6
  400.7 4.2 scatter_fusion.2
  405.0 6.2 copy.241
  411.2 6.4 convert_element_type.212
  417.5 8.5 copy.242
  426.1 7.8 convert_element_type.214
  436.2 6.1 fusion.334
  442.4 4.6 all-to-all-start.7
  447.0 5.2 fusion.7
  458.8 3.3 fusion.63
  462.0 3.3 convert_element_type.220
  465.3 5.0 copy.391
  470.3 5.5 convert_element_type.222
  475.8 3.5 copy.245
  479.2 3.6 all-to-all-start.8
  483.1 48.8 %all-to-all-done.8 = bf16[2,512,1024]{2,0,1:T(2,128)(2,1)S(1)} async-done(((bf16[2,512,1024]{2,0,1:T(2,128)(2,1)}), bf16[2,512,1024]{2,0,1:T(2,128)(2,1)S(1)}, u32[]{:S(2)}, u32[]{:S(2)}) %all-to-all-start.8) | async-done | bytes 2097184 | tf_op jit(solution)/shard_map/all_to_all | solution.py:199
  551.2 3.5 fusion.95
  555.3 3.2 fusion.92
  559.5 17.8 %copy.260 = bf16[2,4096,128]{2,0,1:T(2,128)(2,1)S(1)} copy(bf16[2,4096,128]{2,1,0:T(8,128)(2,1)S(1)} %maximum_bitcast_fusion) | data formatting | bytes 4194304 | tf_op jit(solution)/shard_map/convert_element_type | solution.py:206
  577.3 30.2 %all_to_all.147 = bf16[2,4096,128]{2,0,1:T(2,128)(2,1)S(1)} all-to-all(bf16[2,4096,128]{2,0,1:T(2,128)(2,1)S(1)} %copy.260), channel_id=1, replica_groups=mesh['vis'=8,'wav'=4] {'vis'}, dimensions={1} | all-to-all | bytes 4194304 | tf_op jit(solution)/shard_map/all_to_all | solution.py:205
  610.3 5.0 copy.263
  615.4 50.4 %all_to_all.148 = bf16[2,512,1024]{2,0,1:T(2,128)(2,1)S(1)} all-to-all(bf16[2,512,1024]{2,0,1:T(2,128)(2,1)S(1)} %copy.263), channel_id=1, replica_groups=mesh['vis'=8,'wav'=4] {'wav'}, dimensions={1} | all-to-all | bytes 4194304 | tf_op jit(solution)/shard_map/all_to_all | solution.py:204
  667.7 3.4 copy.265
  682.0 3.4 fusion.98
  686.1 27.8 %all_to_all.149 = bf16[128,4,1024]{0,2,1:T(8,128)(2,1)S(1)} all-to-all(bf16[128,4,1024]{0,2,1:T(8,128)(2,1)S(1)} %bitcast.254), channel_id=1, replica_groups=mesh['vis'=8,'wav'=4] {'wav'}, dimensions={1} | all-to-all | bytes 2097152 | tf_op jit(solution)/shard_map/all_to_all | solution.py:218
  718.4 3.3 bitcast_subtract_fusion
  723.6 145.7 %all-gather.2.cloned.1.call-done = f32[512,4096]{1,0:T(8,128)} async-done(((f32[512,1024]{1,0:T(8,128)}), f32[512,4096]{1,0:T(8,128)}) %all-gather.2.cloned.1.call-update) | async-done | bytes 8388624 | tf_op jit(solution)/shard_map/all_gather | solution.py:225
  869.3 11.0 %fusion.2 = f32[64,8,32,128]{3,1,2,0:T(8,128)} fusion(s32[]{:T(128)S(6)} %select_n.151, f32[512,4096]{1,0:T(8,128)} %all-gather.2.cloned.1.call-done), kind=kLoop, calls=%fused_computation.12 | loop fusion | flops 2097152 | bytes 16777220
  880.3 5.2 copy.287
  885.6 13.3 %fusion.5 = f32[256,2,32,128]{3,0,2,1:T(8,128)S(1)} fusion(f32[128,128,1,1]{1,0,3,2:T(8,128)S(1)} %copy-done.9, f32[256,2,32,128]{3,2,1,0:T(8,128)S(1)} %bitcast.221), kind=kOutput, calls=%fused_computation.16 | convolution fusion | flops 3221225472 | bytes 16842752 | tf_op jit(solution)/shard_map/rgj,kj->rgk/dot_general | solution.py:34
  902.8 4.9 copy.277
  907.7 13.4 %fusion.3 = f32[512,32,128]{0,2,1:T(8,128)} fusion(f32[128,128,1]{1,0,2:T(8,128)S(1)} %copy-done.8, f32[512,32,128]{2,1,0:T(8,128)S(1)} %bitcast.222), kind=kOutput, calls=%fused_computation.14 | convolution fusion | flops 3221225472 | bytes 16842752 | tf_op jit(solution)/shard_map/rgk,kj->rgj/dot_general | solution.py:43
  921.1 9.2 copy.280
  930.3 11.0 %fusion = f32[512,4096]{1,0:T(8,128)} fusion(s32[]{:T(128)S(6)} %select_n.153, f32[512,4096]{1,0:T(8,128)} %copy.280), kind=kLoop, calls=%fused_computation.10 | loop fusion | flops 2097152 | bytes 16777220 | tf_op jit(solution)/shard_map/jit(_roll_dynamic)/concatenate | solution.py:44
  941.4 3.7 all-to-all-start.12
  945.1 5.5 all-to-all-done.12
  951.8 132.6 %reduce-scatter.2.cloned.1.call-done = f32[512,1024]{1,0:T(8,128)} async-done(((f32[512,4096]{1,0:T(8,128)}), f32[512,1024]{1,0:T(8,128)}) %reduce-scatter.2.cloned.1.call-update) | async-done | bytes 2097168 | tf_op jit(solution)/shard_map/reduce_scatter | solution.py:227
  (114 shorter events, 91.4 us)
Async XLA Ops:
  7.2 54.6 %all-to-all-start.2 = ((f32[4,128,1024]{2,1,0:T(8,128)}), f32[4,128,1024]{2,1,0:T(8,128)S(1)}, u32[]{:S(2)}, u32[]{:S(2)}) async-start(f32[4,128,1024]{2,1,0:T(8,128)} %bitcast.244), calls=%async_computation.2 | async-start | bytes 4194304 | tf_op jit(solution)/shard_map/all_to_all | solution.py:151
  61.7 1.3 copy-start.4
  171.2 5.0 copy-start.12
  171.2 5.0 copy-start.11
  171.2 97.9 %all-to-all-start.4 = ((f32[2,1024,512]{1,0,2:T(2,128)}), f32[2,1024,512]{1,0,2:T(2,128)}, u32[]{:S(2)}, u32[]{:S(2)}) async-start(f32[2,1024,512]{1,0,2:T(2,128)} %copy.223), calls=%async_computation.4 | async-start | bytes 8388608 | tf_op jit(solution)/shard_map/all_to_all | solution.py:157
  176.2 11.4 %copy-start.6 = (bf16[32,64,256]{2,1,0:T(8,128)(2,1)S(1)}, bf16[32,64,256]{2,1,0:T(8,128)(2,1)}, u32[]{:S(2)}) copy-start(bf16[32,64,256]{2,1,0:T(8,128)(2,1)} %param.11) | copy-start | bytes 3145732
  189.3 88.7 %copy-start.1 = (bf16[64,64,256]{2,1,0:T(8,128)(2,1)}, bf16[64,64,256]{2,1,0:T(8,128)(2,1)S(1)}, u32[]{:S(2)}) copy-start(bf16[64,64,256]{2,1,0:T(8,128)(2,1)S(1)} %scatter_fusion) | copy-start | bytes 6291460
  269.1 33.6 %all-to-all-start = ((bf16[8,8,1]{1,2,0:T(2,128)(2,1)}), bf16[8,8,1]{1,2,0:T(2,128)(2,1)S(1)}, u32[]{:S(2)}, u32[]{:S(2)}) async-start(bf16[8,8,1]{1,2,0:T(2,128)(2,1)} %all_to_all.132), calls=%async_computation | async-start | bytes 8192 | tf_op jit(solution)/shard_map/all_to_all | solution.py:144
  302.7 39.6 %all-to-all-start.1 = ((bf16[64,64,256]{2,1,0:T(8,128)(2,1)}), bf16[64,64,256]{2,1,0:T(8,128)(2,1)}, u32[]{:S(2)}, u32[]{:S(2)}) async-start(bf16[64,64,256]{2,1,0:T(8,128)(2,1)} %copy-done.1), calls=%async_computation.1 | async-start | bytes 4194304 | tf_op jit(solution)/shard_map/all_to_all | solution.py:141
  315.0 1.6 copy-start
  342.4 53.5 %all-to-all-start.5 = ((bf16[2,128,4096]{1,0,2:T(2,128)(2,1)}), bf16[2,128,4096]{1,0,2:T(2,128)(2,1)}, u32[]{:S(2)}, u32[]{:S(2)}) async-start(bf16[2,128,4096]{1,0,2:T(2,128)(2,1)} %copy.240), calls=%async_computation.5 | async-start | bytes 4194304 | tf_op jit(solution)/shard_map/all_to_all | solution.py:171
  346.9 1.2 copy-start.7
  349.7 1.3 copy-start.2
  351.0 49.6 %copy-start.10 = (bf16[32,2,256]{2,1,0:T(2,128)(2,1)S(1)}, bf16[32,2,256]{2,1,0:T(2,128)(2,1)}, u32[]{:S(2)}) copy-start(bf16[32,2,256]{2,1,0:T(2,128)(2,1)} %param.13) | copy-start | bytes 98308
  395.9 46.5 %all-to-all-start.6 = ((bf16[64,64,256]{2,1,0:T(8,128)(2,1)}), bf16[64,64,256]{2,1,0:T(8,128)(2,1)S(1)}, u32[]{:S(2)}, u32[]{:S(2)}) async-start(bf16[64,64,256]{2,1,0:T(8,128)(2,1)} %copy-done.2), calls=%async_computation.6 | async-start | bytes 4194304 | tf_op jit(solution)/shard_map/all_to_all | solution.py:142
  442.4 9.9 all-to-all-start.7
  479.2 52.7 %all-to-all-start.8 = ((bf16[2,512,1024]{2,0,1:T(2,128)(2,1)}), bf16[2,512,1024]{2,0,1:T(2,128)(2,1)S(1)}, u32[]{:S(2)}, u32[]{:S(2)}) async-start(bf16[2,512,1024]{2,0,1:T(2,128)(2,1)} %copy.245), calls=%async_computation.8 | async-start | bytes 4194304 | tf_op jit(solution)/shard_map/all_to_all | solution.py:199
  482.9 386.5 %all-gather.2.cloned.1.call-start = ((), (), s32[]{:S(2)}) async-start(), calls=%async_computation.14 | async-start | bytes 10485760 | tf_op jit(solution)/shard_map/all_gather | solution.py:225
  540.6 1.6 copy-start.5
  715.4 3.1 copy-start.3
  721.7 0.7 copy-start.13
  721.7 362.7 %reduce-scatter.2.cloned.1.call-start = ((), (), s32[]{:S(2)}) async-start(), calls=%async_computation.15 | async-start | bytes 10485760 | tf_op jit(solution)/shard_map/reduce_scatter | solution.py:227
  880.3 5.3 copy-start.9
  902.8 4.9 copy-start.8
  941.4 9.2 all-to-all-start.12
Sparse Core Ops, SparseCore 0:
  721.9 147.4 all-gather.1
  941.5 142.8 reduce-scatter.1
where the time goes:
time: 1110 us; the launch traced here: 1100 us
  waiting for transfers between devices  505 us (45%)
  local copies, waits for them, and re-layouts  205 us (18%)
  blocking collectives  161 us (15%)
  matrix products  126 us (11%)
  other arithmetic  42.6 us (4%)
  starting transfers between devices  39.5 us (4%)
  between operations  16 us (1%)
    all_gather x1, waiting for transfers between devices, shards(): gathered = lax.all_gather(estimate - gradient, 'wav', axis=1, tiled=True)  146 us
    reduce_scatter x1, waiting for transfers between devices, shards(): lax.psum_scatter(single, 'wav', scatter_dimension=1, tiled=True)  133 us
    all_to_all x1, waiting for transfers between devices, shards(): lax.all_to_all(lax.all_to_all(stacked, 'vis', split_axis=2, concat_axis=1...  79.8 us
    all_to_all x1, blocking collectives, shards(): lax.all_to_all(stacked, 'vis', split_axis=2, concat_axis=1, tiled=True)  52.6 us
    all_to_all x1, blocking collectives, shards(): lax.all_to_all(lax.all_to_all(stacked.astype(jnp.bfloat16), 'vis', split_...  50.4 us
    all_to_all x1, waiting for transfers between devices, shards(): lax.all_to_all(grid_grad.astype(jnp.bfloat16), 'wav', split_axis=1, conca...  48.8 us
    all_to_all x1, waiting for transfers between devices, shards(): lax.all_to_all(estimate, 'wav', split_axis=0, concat_axis=1, tiled=True)  47.7 us
    all_to_all x1, waiting for transfers between devices, shards(): lax.all_to_all(jnp.stack([real_part, imag_part], 0).astype(jnp.bfloat16),...  44.9 us
  transfers between devices with their start and end apart: 11, of which 7 were waited for; matrix products, arithmetic and copies ran while one was open for 12% of the time, Pallas kernels for 0%

commit v1 on v0

--- a/solution.py
+++ b/solution.py
@@ -10,6 +10,12 @@
 FA = 64
 FB = 64
 HIGHEST = lax.Precision.HIGHEST
+
+
+def joined_along(tiles, dim):
+    tiles = jnp.moveaxis(tiles, 0, dim)
+    shape = tiles.shape
+    return tiles.reshape(*shape[:dim], shape[dim] * shape[dim + 1], *shape[dim + 2 :])
 
 
 def haar_table():
@@ -222,7 +228,15 @@
         concat_axis=0,
         tiled=True,
     ).astype(jnp.float32)
-    gathered = lax.all_gather(estimate - gradient, "wav", axis=1, tiled=True)
+    array = estimate - gradient
+    size = lax.axis_size("wav")
+    right = [(i, (i + 1) % size) for i in range(size)]
+    pieces = [array]
+    while len(pieces) < size:
+        pieces.append(lax.ppermute(pieces[-1], "wav", right))
+    place = lax.axis_index("wav")
+    pieces = jnp.stack(pieces)[(place - jnp.arange(size)) % size]
+    gathered = joined_along(pieces, 1)
     single = basis_prox(gathered, wav_index, thresholds[wav_index], table)
     estimate = lax.psum_scatter(single, "wav", scatter_dimension=1, tiled=True) * (1.0 / wav_count)
     returned = lax.all_to_all(misfit, "vis", split_axis=0, concat_axis=0, tiled=True)

time: 1110 us -> 1130 us (1.018)
  local copies, waits for them, and re-layouts: 205 us -> 231 us
    all_gather x1 -> x0, waiting for transfers between devices: 146 us -> none  [shards(): gathered = lax.all_gather(estimate - gradient, 'wav', axis=1, tiled=True)]
    ppermute x0 -> x3, waiting for transfers between devices: none -> 140 us  [shards(): pieces.append(lax.ppermute(pieces[-1], 'wav', right))]
  transfers between devices with their start and end apart: 11 -> 13, of which waited for: 7 -> 9; matrix products, arithmetic and copies ran while one was open for 12% -> 12% of each run, Pallas kernels for 0% -> 0%
where the time goes in v1:
time: 1130 us; the launch traced here: 1120 us
  waiting for transfers between devices  498 us (44%)
  local copies, waits for them, and re-layouts  231 us (20%)
  blocking collectives  161 us (14%)
  matrix products  126 us (11%)
  other arithmetic  45.9 us (4%)
  starting transfers between devices  39.4 us (3%)
  between operations  16 us (1%)
    ppermute x3, waiting for transfers between devices, shards(): pieces.append(lax.ppermute(pieces[-1], 'wav', right))  140 us
    reduce_scatter x1, waiting for transfers between devices, shards(): lax.psum_scatter(single, 'wav', scatter_dimension=1, tiled=True)  132 us
    all_to_all x1, waiting for transfers between devices, shards(): lax.all_to_all(lax.all_to_all(stacked, 'vis', split_axis=2, concat_axis=1...  79.8 us
    all_to_all x1, blocking collectives, shards(): lax.all_to_all(stacked, 'vis', split_axis=2, concat_axis=1, tiled=True)  52.6 us
    all_to_all x1, blocking collectives, shards(): lax.all_to_all(lax.all_to_all(stacked.astype(jnp.bfloat16), 'vis', split_...  50.4 us
    all_to_all x1, waiting for transfers between devices, shards(): lax.all_to_all(grid_grad.astype(jnp.bfloat16), 'wav', split_axis=1, conca...  48.8 us
    all_to_all x1, waiting for transfers between devices, shards(): lax.all_to_all(estimate, 'wav', split_axis=0, concat_axis=1, tiled=True)  47.7 us
    all_to_all x1, waiting for transfers between devices, shards(): lax.all_to_all(jnp.stack([real_part, imag_part], 0).astype(jnp.bfloat16),...  44.9 us
  transfers between devices with their start and end apart: 13, of which 9 were waited for; matrix products, arithmetic and copies ran while one was open for 12% of the time, Pallas kernels for 0%

profile of v1, /device:TPU:0, one launch (start us, length us, event | category | flops | bytes accessed | tf_op | source)
XLA Modules:
  0.0 1117.6 jit_solution(16971265015000599979)
XLA Ops:
  7.2 6.4 all-to-all-start.2
  14.0 47.7 %all-to-all-done.2 = f32[4,128,1024]{2,1,0:T(8,128)S(1)} async-done(((f32[4,128,1024]{2,1,0:T(8,128)}), f32[4,128,1024]{2,1,0:T(8,128)S(1)}, u32[]{:S(2)}, u32[]{:S(2)}) %all-to-all-start.2) | async-done | bytes 2097184 | tf_op jit(solution)/shard_map/all_to_all | solution.py:157
  68.1 4.2 subtract_bitcast_fusion
  75.4 3.4 fusion.52
  88.0 15.6 %copy.225 = f32[2,128,4096]{1,0,2:T(2,128)S(1)} copy(f32[2,128,4096]{1,2,0:T(8,128)S(1)} %pad_maximum_fusion.2) | data formatting | bytes 8388608 | tf_op jit(solution)/shard_map/stack | solution.py:162
  103.6 52.6 %all_to_all.146 = f32[2,128,4096]{1,0,2:T(2,128)S(1)} all-to-all(f32[2,128,4096]{1,0,2:T(2,128)S(1)} %copy.225), channel_id=1, replica_groups=mesh['vis'=8,'wav'=4] {'vis'}, dimensions={2} | all-to-all | bytes 8388608 | tf_op jit(solution)/shard_map/all_to_all | solution.py:164
  158.5 5.3 copy.227
  163.8 7.4 copy.228
  171.2 5.0 all-to-all-start.4
  176.6 10.1 scatter_custom_fusion
  189.3 79.8 %all-to-all-done.4 = f32[2,1024,512]{1,0,2:T(2,128)} async-done(((f32[2,1024,512]{1,0,2:T(2,128)}), f32[2,1024,512]{1,0,2:T(2,128)}, u32[]{:S(2)}, u32[]{:S(2)}) %all-to-all-start.4) | async-done | bytes 4194336 | tf_op jit(solution)/shard_map/all_to_all | solution.py:163
  269.1 3.3 all-to-all-start
  272.5 5.5 copy.229
  278.0 5.4 copy.230
  286.2 3.3 fusion.42
  289.6 3.3 fusion.44
  293.2 3.4 fusion.69
  296.5 6.3 fusion.18
  302.8 4.4 all-to-all-start.1
  307.2 4.6 fusion.34
  319.8 3.7 fusion.85
  324.3 18.1 %copy.245 = bf16[2,128,4096]{1,0,2:T(2,128)(2,1)} copy(bf16[2,128,4096]{1,2,0:T(8,128)(2,1)S(1)} %pad_maximum_fusion.3) | data formatting | bytes 4194304 | tf_op jit(solution)/shard_map/stack | solution.py:178
  342.4 4.5 all-to-all-start.5
  351.1 44.9 %all-to-all-done.5 = bf16[2,128,4096]{1,0,2:T(2,128)(2,1)} async-done(((bf16[2,128,4096]{1,0,2:T(2,128)(2,1)}), bf16[2,128,4096]{1,0,2:T(2,128)(2,1)}, u32[]{:S(2)}, u32[]{:S(2)}) %all-to-all-start.5) | async-done | bytes 2097184 | tf_op jit(solution)/shard_map/all_to_all | solution.py:177
  396.0 4.1 all-to-all-start.6
  400.7 4.2 scatter_fusion.2
  405.1 6.2 copy.246
  411.3 6.3 convert_element_type.212
  417.6 8.6 copy.247
  426.2 7.8 convert_element_type.214
  436.3 6.2 fusion.335
  442.4 4.6 all-to-all-start.7
  447.1 5.2 fusion.6
  458.8 3.3 fusion.62
  465.3 5.0 copy.398
  470.4 5.5 convert_element_type.222
  475.8 3.5 copy.250
  479.3 3.6 all-to-all-start.8
  483.2 48.8 %all-to-all-done.8 = bf16[2,512,1024]{2,0,1:T(2,128)(2,1)S(1)} async-done(((bf16[2,512,1024]{2,0,1:T(2,128)(2,1)}), bf16[2,512,1024]{2,0,1:T(2,128)(2,1)S(1)}, u32[]{:S(2)}, u32[]{:S(2)}) %all-to-all-start.8) | async-done | bytes 2097184 | tf_op jit(solution)/shard_map/all_to_all | solution.py:205
  551.2 3.5 fusion.94
  559.5 17.8 %copy.265 = bf16[2,4096,128]{2,0,1:T(2,128)(2,1)S(1)} copy(bf16[2,4096,128]{2,1,0:T(8,128)(2,1)S(1)} %maximum_bitcast_fusion) | data formatting | bytes 4194304 | tf_op jit(solution)/shard_map/convert_element_type | solution.py:212
  577.4 30.2 %all_to_all.147 = bf16[2,4096,128]{2,0,1:T(2,128)(2,1)S(1)} all-to-all(bf16[2,4096,128]{2,0,1:T(2,128)(2,1)S(1)} %copy.265), channel_id=1, replica_groups=mesh['vis'=8,'wav'=4] {'vis'}, dimensions={1} | all-to-all | bytes 4194304 | tf_op jit(solution)/shard_map/all_to_all | solution.py:211
  610.4 5.0 copy.268
  615.4 50.4 %all_to_all.148 = bf16[2,512,1024]{2,0,1:T(2,128)(2,1)S(1)} all-to-all(bf16[2,512,1024]{2,0,1:T(2,128)(2,1)S(1)} %copy.268), channel_id=1, replica_groups=mesh['vis'=8,'wav'=4] {'wav'}, dimensions={1} | all-to-all | bytes 4194304 | tf_op jit(solution)/shard_map/all_to_all | solution.py:210
  667.8 3.4 copy.270
  682.0 3.4 fusion.97
  686.2 27.8 %all_to_all.149 = bf16[128,4,1024]{0,2,1:T(8,128)(2,1)S(1)} all-to-all(bf16[128,4,1024]{0,2,1:T(8,128)(2,1)S(1)} %bitcast.265), channel_id=1, replica_groups=mesh['vis'=8,'wav'=4] {'wav'}, dimensions={1} | all-to-all | bytes 2097152 | tf_op jit(solution)/shard_map/all_to_all | solution.py:224
  722.0 47.7 %collective-permute-done = f32[512,1024]{1,0:T(8,128)S(1)} collective-permute-done((f32[512,1024]{1,0:T(8,128)S(1)}, f32[512,1024]{1,0:T(8,128)S(1)}, u32[]{:S(2)}, u32[]{:S(2)}) %collective-permute-start) | collective-permute-done | bytes 2097184 | tf_op jit(solution)/shard_map/ppermute | solution.py:236
  769.7 47.1 %collective-permute-done.1 = f32[512,1024]{1,0:T(8,128)} collective-permute-done((f32[512,1024]{1,0:T(8,128)S(1)}, f32[512,1024]{1,0:T(8,128)}, u32[]{:S(2)}, u32[]{:S(2)}) %collective-permute-start.1) | collective-permute-done | bytes 2097184 | tf_op jit(solution)/shard_map/ppermute | solution.py:236
  818.1 45.2 %collective-permute-done.2 = f32[512,1024]{1,0:T(8,128)} collective-permute-done((f32[512,1024]{1,0:T(8,128)}, f32[512,1024]{1,0:T(8,128)}, u32[]{:S(2)}, u32[]{:S(2)}) %collective-permute-start.2) | collective-permute-done | bytes 2097184 | tf_op jit(solution)/shard_map/ppermute | solution.py:236
  863.4 5.7 pad_maximum_fusion
  869.0 7.7 gather_fusion.1
  876.7 8.8 copy.281
  885.5 9.9 fusion.1
  895.4 8.9 copy.282
  904.3 5.2 copy.294
  909.6 13.3 %fusion.4 = f32[256,2,32,128]{3,0,2,1:T(8,128)S(1)} fusion(f32[128,128,1,1]{1,0,3,2:T(8,128)S(1)} %copy-done.10, f32[256,2,32,128]{3,2,1,0:T(8,128)S(1)} %bitcast.228), kind=kOutput, calls=%fused_computation.17 | convolution fusion | flops 3221225472 | bytes 16842752 | tf_op jit(solution)/shard_map/rgj,kj->rgk/dot_general | solution.py:40
  926.8 4.9 copy.284
  931.7 13.4 %fusion.2 = f32[512,32,128]{0,2,1:T(8,128)} fusion(f32[128,128,1]{1,0,2:T(8,128)S(1)} %copy-done.9, f32[512,32,128]{2,1,0:T(8,128)S(1)} %bitcast.231), kind=kOutput, calls=%fused_computation.15 | convolution fusion | flops 3221225472 | bytes 16842752 | tf_op jit(solution)/shard_map/rgk,kj->rgj/dot_general | solution.py:49
  945.1 9.2 copy.287
  954.3 11.0 fusion
  965.4 3.4 all-to-all-start.12
  968.8 5.4 all-to-all-done.12
  975.4 131.6 %reduce-scatter.2.cloned.1.call-done = f32[512,1024]{1,0:T(8,128)} async-done(((f32[512,4096]{1,0:T(8,128)}), f32[512,1024]{1,0:T(8,128)}) %reduce-scatter.2.cloned.1.call-update) | async-done | bytes 2097168 | tf_op jit(solution)/shard_map/reduce_scatter | solution.py:241
  (125 shorter events, 110.6 us)
Async XLA Ops:
  7.2 54.6 %all-to-all-start.2 = ((f32[4,128,1024]{2,1,0:T(8,128)}), f32[4,128,1024]{2,1,0:T(8,128)S(1)}, u32[]{:S(2)}, u32[]{:S(2)}) async-start(f32[4,128,1024]{2,1,0:T(8,128)} %bitcast.254), calls=%async_computation.2 | async-start | bytes 4194304 | tf_op jit(solution)/shard_map/all_to_all | solution.py:157
  61.7 1.3 copy-start.4
  171.2 5.0 copy-start.13
  171.2 5.0 copy-start.12
  171.2 97.9 %all-to-all-start.4 = ((f32[2,1024,512]{1,0,2:T(2,128)}), f32[2,1024,512]{1,0,2:T(2,128)}, u32[]{:S(2)}, u32[]{:S(2)}) async-start(f32[2,1024,512]{1,0,2:T(2,128)} %copy.228), calls=%async_computation.4 | async-start | bytes 8388608 | tf_op jit(solution)/shard_map/all_to_all | solution.py:163
  176.2 11.4 %copy-start.7 = (bf16[32,64,256]{2,1,0:T(8,128)(2,1)S(1)}, bf16[32,64,256]{2,1,0:T(8,128)(2,1)}, u32[]{:S(2)}) copy-start(bf16[32,64,256]{2,1,0:T(8,128)(2,1)} %param.11) | copy-start | bytes 3145732
  189.3 88.7 %copy-start.1 = (bf16[64,64,256]{2,1,0:T(8,128)(2,1)}, bf16[64,64,256]{2,1,0:T(8,128)(2,1)S(1)}, u32[]{:S(2)}) copy-start(bf16[64,64,256]{2,1,0:T(8,128)(2,1)S(1)} %scatter_fusion) | copy-start | bytes 6291460
  269.1 33.6 %all-to-all-start = ((bf16[8,8,1]{1,2,0:T(2,128)(2,1)}), bf16[8,8,1]{1,2,0:T(2,128)(2,1)S(1)}, u32[]{:S(2)}, u32[]{:S(2)}) async-start(bf16[8,8,1]{1,2,0:T(2,128)(2,1)} %all_to_all.132), calls=%async_computation | async-start | bytes 8192 | tf_op jit(solution)/shard_map/all_to_all | solution.py:150
  302.8 39.6 %all-to-all-start.1 = ((bf16[64,64,256]{2,1,0:T(8,128)(2,1)}), bf16[64,64,256]{2,1,0:T(8,128)(2,1)}, u32[]{:S(2)}, u32[]{:S(2)}) async-start(bf16[64,64,256]{2,1,0:T(8,128)(2,1)} %copy-done.1), calls=%async_computation.1 | async-start | bytes 4194304 | tf_op jit(solution)/shard_map/all_to_all | solution.py:147
  315.1 1.6 copy-start
  342.4 53.5 %all-to-all-start.5 = ((bf16[2,128,4096]{1,0,2:T(2,128)(2,1)}), bf16[2,128,4096]{1,0,2:T(2,128)(2,1)}, u32[]{:S(2)}, u32[]{:S(2)}) async-start(bf16[2,128,4096]{1,0,2:T(2,128)(2,1)} %copy.245), calls=%async_computation.5 | async-start | bytes 4194304 | tf_op jit(solution)/shard_map/all_to_all | solution.py:177
  346.9 1.2 copy-start.8
  349.7 1.3 copy-start.2
  351.1 49.6 %copy-start.11 = (bf16[32,2,256]{2,1,0:T(2,128)(2,1)S(1)}, bf16[32,2,256]{2,1,0:T(2,128)(2,1)}, u32[]{:S(2)}) copy-start(bf16[32,2,256]{2,1,0:T(2,128)(2,1)} %param.13) | copy-start | bytes 98308
  396.0 46.5 %all-to-all-start.6 = ((bf16[64,64,256]{2,1,0:T(8,128)(2,1)}), bf16[64,64,256]{2,1,0:T(8,128)(2,1)S(1)}, u32[]{:S(2)}, u32[]{:S(2)}) async-start(bf16[64,64,256]{2,1,0:T(8,128)(2,1)} %copy-done.2), calls=%async_computation.6 | async-start | bytes 4194304 | tf_op jit(solution)/shard_map/all_to_all | solution.py:148
  442.4 9.9 all-to-all-start.7
  479.3 52.7 %all-to-all-start.8 = ((bf16[2,512,1024]{2,0,1:T(2,128)(2,1)}), bf16[2,512,1024]{2,0,1:T(2,128)(2,1)S(1)}, u32[]{:S(2)}, u32[]{:S(2)}) async-start(bf16[2,512,1024]{2,0,1:T(2,128)(2,1)} %copy.250), calls=%async_computation.8 | async-start | bytes 4194304 | tf_op jit(solution)/shard_map/all_to_all | solution.py:205
  482.9 624.1 %reduce-scatter.2.cloned.1.call-start = ((), (), s32[]{:S(2)}) async-start(), calls=%async_computation.14 | async-start | bytes 10485760 | tf_op jit(solution)/shard_map/reduce_scatter | solution.py:241
  540.6 1.6 copy-start.5
  715.4 3.0 copy-start.3
  718.5 98.4 %copy-start.14 = (f32[4]{0:T(128)S(1)}, f32[4]{0:T(128)}, u32[]{:S(2)}) copy-start(f32[4]{0:T(128)} %param.16) | copy-start | bytes 52
  720.5 1.3 copy-start.6
  721.8 47.9 %collective-permute-start = (f32[512,1024]{1,0:T(8,128)S(1)}, f32[512,1024]{1,0:T(8,128)S(1)}, u32[]{:S(2)}, u32[]{:S(2)}) collective-permute-start(f32[512,1024]{1,0:T(8,128)S(1)} %bitcast_subtract_fusion), channel_id=1, source_target_pairs={{0,1},{1,2},{2,3},{3,0},{4,5},{5,6},{6,7},{7,4},{8,9},{9,10},{10,1... | collective-permute-start | bytes 6291464 | tf_op jit(solution)/shard_map/ppermute | solution.py:236
  769.7 47.2 %collective-permute-start.1 = (f32[512,1024]{1,0:T(8,128)S(1)}, f32[512,1024]{1,0:T(8,128)}, u32[]{:S(2)}, u32[]{:S(2)}) collective-permute-start(f32[512,1024]{1,0:T(8,128)S(1)} %collective-permute-done), channel_id=1, source_target_pairs={{0,1},{1,2},{2,3},{3,0},{4,5},{5,6},{6,7},{7,4},{8,9},{9,10},{10,1... | collective-permute-start | bytes 6291464 | tf_op jit(solution)/shard_map/ppermute | solution.py:236
  816.9 46.5 %collective-permute-start.2 = (f32[512,1024]{1,0:T(8,128)}, f32[512,1024]{1,0:T(8,128)}, u32[]{:S(2)}, u32[]{:S(2)}) collective-permute-start(f32[512,1024]{1,0:T(8,128)} %collective-permute-done.1), channel_id=1, source_target_pairs={{0,1},{1,2},{2,3},{3,0},{4,5},{5,6},{6,7},{7,4},{8,9},{9,10},{10,1... | collective-permute-start | bytes 6291464 | tf_op jit(solution)/shard_map/ppermute | solution.py:236
  904.3 5.3 copy-start.10
  926.8 4.9 copy-start.9
  965.4 8.8 all-to-all-start.12
Sparse Core Ops, SparseCore 0:
  965.5 141.5 reduce-scatter.1
